TPU v7x, 32 devices: a whole 2x2x4 slice. The times are simulated.
32 devices in a mesh: rep: 2 (over y), fsdp: 4 (over z), seq: 4 (over x, core).
Axes of the slice: x: 2, y: 2, z: 4, core: 2. Of those that a mesh axis runs over, the one named last changes fastest.
Arguments:
- latents: bfloat16 [8, 1024, 1152], P(('rep', 'fsdp'), 'seq'), may hold values from -6 to 6
- cond: bfloat16 [8, 1152], P(('rep', 'fsdp')), may hold values from -6 to 6
- w_ada: bfloat16 [1152, 6912], P(('fsdp', 'seq')), may hold values from -0.25 to 0.25
- b_ada: bfloat16 [6912], P(('fsdp', 'seq')), may hold values from -3 to 3
- w_qkv: bfloat16 [1152, 3456], P(('fsdp', 'seq')), may hold values from -0.1875 to 0.1875
- b_qv: bfloat16 [2304], P(('fsdp', 'seq')), may hold values from -3 to 3
- w_out: bfloat16 [1152, 1152], P(('fsdp', 'seq')), may hold values from -1.5 to 1.5
- b_out: bfloat16 [1152], P(('fsdp', 'seq')), may hold values from -3 to 3
- w_one: bfloat16 [1152, 4608], P(('fsdp', 'seq')), may hold values from -0.1875 to 0.1875
- b_one: bfloat16 [4608], P(('fsdp', 'seq')), may hold values from -3 to 3
- w_two: bfloat16 [4608, 1152], P(('fsdp', 'seq')), may hold values from -0.09375 to 0.09375
- b_two: bfloat16 [1152], P(('fsdp', 'seq')), may hold values from -3 to 3
- cotangent: bfloat16 [8, 1024, 1152], P(('rep', 'fsdp'), 'seq'), may hold values from -6 to 6
Outputs:
- block_out: bfloat16 [8, 1024, 1152], P(('rep', 'fsdp'), 'seq')
- grad_latents: float32 [8, 1024, 1152], P(('rep', 'fsdp'), 'seq')
- grad_cond: float32 [8, 1152], P(('rep', 'fsdp'))
- grad_w_ada: float32 [1152, 6912], P(('fsdp', 'seq'))
- grad_b_ada: float32 [6912], P(('fsdp', 'seq'))
- grad_w_qkv: float32 [1152, 3456], P(('fsdp', 'seq'))
- grad_b_qv: float32 [2304], P(('fsdp', 'seq'))
- grad_w_out: float32 [1152, 1152], P(('fsdp', 'seq'))
- grad_b_out: float32 [1152], P(('fsdp', 'seq'))
- grad_w_one: float32 [1152, 4608], P(('fsdp', 'seq'))
- grad_b_one: float32 [4608], P(('fsdp', 'seq'))
- grad_w_two: float32 [4608, 1152], P(('fsdp', 'seq'))
- grad_b_two: float32 [1152], P(('fsdp', 'seq'))
All inputs are finite; a program needn't handle non-finite values.
Results may differ from a plain program's by a relative error of at most 0.014.
The roundings to bfloat16 on the way count: a program that leaves them out, or rounds other values in their place, can miss the bound.
Values may be sent and summed in bfloat16 or wider, within the bound.
A program may use at most 448 MiB of HBM per device.

v0:
```python
import math
import jax
import jax.numpy as jnp
from jax import lax
from jax.sharding import PartitionSpec as P

H = 16
epsilon = 1e-06
gelu_coef = math.sqrt(2.0 / math.pi)


def norm_stats(values):
    center = values - jnp.mean(values, axis=-1, keepdims=True)
    inv_std = lax.rsqrt(jnp.mean(center * center, axis=-1, keepdims=True) + epsilon)
    return (center * inv_std, inv_std)


def norm_back(grad, normed, inv_std):
    return inv_std * (
        grad
        - jnp.mean(grad, axis=-1, keepdims=True)
        - normed * jnp.mean(grad * normed, axis=-1, keepdims=True)
    )


def gelu_tanh(values):
    inner = gelu_coef * (values + 0.044715 * values * values * values)
    return 0.5 * values * (1.0 + jnp.tanh(inner))


def gelu_slope(values):
    inner = gelu_coef * (values + 0.044715 * values * values * values)
    tanh_val = jnp.tanh(inner)
    return 0.5 * (1.0 + tanh_val) + 0.5 * values * (1.0 - tanh_val * tanh_val) * gelu_coef * (
        1.0 + 3.0 * 0.044715 * values * values
    )


def row_dot(left, right):
    return jnp.dot(left, right, preferred_element_type=jnp.float32)


def back_dot(grad, weight):
    return lax.dot_general(
        grad, weight, (((1,), (1,)), ((), ())), preferred_element_type=jnp.float32
    )


def outer_dot(left, grad):
    return lax.dot_general(left, grad, (((0,), (0,)), ((), ())), preferred_element_type=jnp.float32)


def pack_rows(arrays, groups):
    return jnp.concatenate([array.reshape(groups, -1) for array in arrays], axis=1).reshape(-1)


def unpack_rows(flat, layouts, groups):
    pieces = []
    offset = 0
    for layout in layouts:
        amount = math.prod(layout) // groups
        piece = flat[offset : offset + amount].reshape((layout[0] // groups,) + tuple(layout[1:]))
        pieces.append(piece)
        offset = offset + amount
    return pieces


def split_blocks(array, block_len):
    shape = array.shape
    return jnp.moveaxis(
        array.reshape(shape[:2] + (shape[2] // block_len, block_len) + shape[3:]), 2, 0
    )


def join_blocks(array):
    moved = jnp.moveaxis(array, 0, 2)
    shape = moved.shape
    return moved.reshape(shape[:2] + (shape[2] * shape[3],) + shape[4:])


def attention_forward(queries, key_rows, val_rows):
    length = queries.shape[2]
    head_size = queries.shape[3]
    block_len = min(512, length)
    score_scale = head_size ** (-0.5)

    def one_block(query_block):
        scores = (
            jnp.einsum("bhqd,bhkd->bhqk", query_block, key_rows, preferred_element_type=jnp.float32)
            * score_scale
        )
        highest = jnp.max(scores, axis=-1, keepdims=True)
        raised = jnp.exp(scores - highest)
        summed = jnp.sum(raised, axis=-1, keepdims=True)
        probs_low = (raised / summed).astype(jnp.bfloat16)
        result = jnp.einsum(
            "bhqk,bhkd->bhqd", probs_low, val_rows, preferred_element_type=jnp.float32
        )
        return (result.astype(jnp.bfloat16), (highest + jnp.log(summed))[..., 0])

    outputs, log_totals = lax.map(one_block, split_blocks(queries, block_len))
    return (join_blocks(outputs), join_blocks(log_totals))


def attention_backward(queries, key_rows, val_rows, log_totals, grad_out):
    length = queries.shape[2]
    head_size = queries.shape[3]
    block_len = min(512, length)
    score_scale = head_size ** (-0.5)

    def one_block(carried, pieces):
        grad_keys, grad_vals = carried
        query_block, grad_block, lse_block = pieces
        scores = (
            jnp.einsum("bhqd,bhkd->bhqk", query_block, key_rows, preferred_element_type=jnp.float32)
            * score_scale
        )
        attn_probs = jnp.exp(scores - lse_block[..., None])
        grad_probs = jnp.einsum(
            "bhqd,bhkd->bhqk", grad_block, val_rows, preferred_element_type=jnp.float32
        )
        row_inner = jnp.sum(attn_probs * grad_probs, axis=-1, keepdims=True)
        grad_scores = (attn_probs * (grad_probs - row_inner)).astype(jnp.bfloat16)
        grad_query = (
            jnp.einsum("bhqk,bhkd->bhqd", grad_scores, key_rows, preferred_element_type=jnp.float32)
            * score_scale
        )
        grad_keys = (
            grad_keys
            + jnp.einsum(
                "bhqk,bhqd->bhkd", grad_scores, query_block, preferred_element_type=jnp.float32
            )
            * score_scale
        )
        grad_vals = grad_vals + jnp.einsum(
            "bhqk,bhqd->bhkd",
            attn_probs.astype(jnp.bfloat16),
            grad_block,
            preferred_element_type=jnp.float32,
        )
        return ((grad_keys, grad_vals), grad_query)

    zeros_start = jnp.zeros(key_rows.shape, jnp.float32)
    pieces = (
        split_blocks(queries, block_len),
        split_blocks(grad_out, block_len),
        split_blocks(log_totals, block_len),
    )
    (grad_keys, grad_vals), grad_queries = lax.scan(one_block, (zeros_start, zeros_start), pieces)
    return (join_blocks(grad_queries), grad_keys, grad_vals)


def on_device(
    latents, cond, w_ada, b_ada, w_qkv, b_qv, w_out, b_out, w_one, b_one, w_two, b_two, cotangent
):
    latent_count, local_len, width = latents.shape
    token_rows = latent_count * local_len
    head_count = H
    head_size = width // head_count
    seq_count = lax.axis_size("seq")
    group_size = lax.axis_size(("fsdp", "seq"))
    local_heads = head_count // seq_count
    full_len = local_len * seq_count
    owner = lax.axis_index(("fsdp", "seq"))
    own_rows = w_ada.shape[0]
    bias_cols = b_ada.shape[0]
    first_latent = lax.axis_index(("rep", "fsdp")) * latent_count
    cond_float = cond.astype(jnp.float32)
    cond_sigmoid = jax.nn.sigmoid(cond_float)
    silu_cond = (cond_float * cond_sigmoid).astype(jnp.bfloat16)
    silu_every = lax.all_gather(silu_cond, ("rep", "fsdp"), axis=0, tiled=True)
    silu_owned = lax.dynamic_slice_in_dim(silu_every, owner * own_rows, own_rows, 1)
    ada_part = row_dot(silu_owned, w_ada)
    bias_slot = (
        lax.dynamic_slice_in_dim(ada_part, owner * bias_cols, bias_cols, 1)
        + b_ada.astype(jnp.float32)[None, :]
    )
    ada_part = lax.dynamic_update_slice_in_dim(ada_part, bias_slot, owner * bias_cols, 1)
    modulation_every = lax.psum(ada_part, ("fsdp", "seq"))
    modulation = lax.dynamic_slice_in_dim(modulation_every, first_latent, latent_count, 0)
    shift_one, scale_one, gate_one, shift_two, scale_two, gate_two = jnp.split(
        modulation[:, None, :], 6, axis=2
    )
    full_fwd = (
        lax.all_gather(w_qkv, ("fsdp", "seq"), axis=0, tiled=True),
        lax.all_gather(b_qv, ("fsdp", "seq"), axis=0, tiled=True),
        lax.all_gather(w_out, ("fsdp", "seq"), axis=0, tiled=True),
        lax.all_gather(b_out, ("fsdp", "seq"), axis=0, tiled=True),
        lax.all_gather(w_one, ("fsdp", "seq"), axis=0, tiled=True),
        lax.all_gather(b_one, ("fsdp", "seq"), axis=0, tiled=True),
        lax.all_gather(w_two, ("fsdp", "seq"), axis=0, tiled=True),
        lax.all_gather(b_two, ("fsdp", "seq"), axis=0, tiled=True),
    )
    qkv_full, qv_bias, out_full, out_bias, one_full, one_bias, two_full, two_bias = full_fwd
    inputs = latents.astype(jnp.float32)
    normed_one, inv_one = norm_stats(inputs)
    mixed_one = (
        (normed_one * (1.0 + scale_one) + shift_one).astype(jnp.bfloat16).reshape(token_rows, width)
    )
    bias_full = jnp.concatenate(
        [qv_bias[:width], jnp.zeros((width,), jnp.bfloat16), qv_bias[width:]]
    ).astype(jnp.float32)
    projected = (row_dot(mixed_one, qkv_full) + bias_full).astype(jnp.bfloat16)
    token_heads = projected.reshape(latent_count, local_len, 3, head_count, head_size).transpose(
        2, 0, 3, 1, 4
    )
    token_heads = token_heads.reshape(3, latent_count, head_count, local_len * head_size)
    head_tokens = lax.all_to_all(token_heads, "seq", split_axis=2, concat_axis=3, tiled=True)
    head_tokens = head_tokens.reshape(3, latent_count, local_heads, full_len, head_size)
    queries = head_tokens[0]
    key_rows = head_tokens[1]
    val_rows = head_tokens[2]
    attended, log_totals = attention_forward(queries, key_rows, val_rows)
    back_tokens = lax.all_to_all(
        attended.reshape(latent_count, local_heads, full_len * head_size),
        "seq",
        split_axis=2,
        concat_axis=1,
        tiled=True,
    )
    merged = (
        back_tokens.reshape(latent_count, head_count, local_len, head_size)
        .transpose(0, 2, 1, 3)
        .reshape(token_rows, width)
    )
    branch_one = (row_dot(merged, out_full) + out_bias.astype(jnp.float32)).reshape(
        latent_count, local_len, width
    )
    residual = inputs + gate_one * branch_one
    normed_two, inv_two = norm_stats(residual)
    mixed_two = (
        (normed_two * (1.0 + scale_two) + shift_two).astype(jnp.bfloat16).reshape(token_rows, width)
    )
    hidden_pre = row_dot(mixed_two, one_full) + one_bias.astype(jnp.float32)
    hidden_act = gelu_tanh(hidden_pre).astype(jnp.bfloat16)
    branch_two = (row_dot(hidden_act, two_full) + two_bias.astype(jnp.float32)).reshape(
        latent_count, local_len, width
    )
    block_out = (residual + gate_two * branch_two).astype(jnp.bfloat16)
    full_back = (
        lax.all_gather(w_qkv, ("fsdp", "seq"), axis=0, tiled=True),
        lax.all_gather(b_qv, ("fsdp", "seq"), axis=0, tiled=True),
        lax.all_gather(w_out, ("fsdp", "seq"), axis=0, tiled=True),
        lax.all_gather(b_out, ("fsdp", "seq"), axis=0, tiled=True),
        lax.all_gather(w_one, ("fsdp", "seq"), axis=0, tiled=True),
        lax.all_gather(b_one, ("fsdp", "seq"), axis=0, tiled=True),
        lax.all_gather(w_two, ("fsdp", "seq"), axis=0, tiled=True),
        lax.all_gather(b_two, ("fsdp", "seq"), axis=0, tiled=True),
    )
    qkv_back = full_back[0]
    out_back = full_back[2]
    one_back = full_back[4]
    two_back = full_back[6]
    grad_out = cotangent.astype(jnp.float32)
    grad_two = (gate_two * grad_out).astype(jnp.bfloat16).reshape(token_rows, width)
    gate_two_grad = jnp.sum(grad_out * branch_two, axis=1)
    two_w_grad = outer_dot(hidden_act, grad_two)
    two_b_grad = jnp.sum(grad_two, axis=0, dtype=jnp.float32)
    grad_pre = (back_dot(grad_two, two_back) * gelu_slope(hidden_pre)).astype(jnp.bfloat16)
    one_w_grad = outer_dot(mixed_two, grad_pre)
    one_b_grad = jnp.sum(grad_pre, axis=0, dtype=jnp.float32)
    grad_mixed_two = back_dot(grad_pre, one_back).reshape(latent_count, local_len, width)
    shift_two_grad = jnp.sum(grad_mixed_two, axis=1)
    scale_two_grad = jnp.sum(grad_mixed_two * normed_two, axis=1)
    grad_resid = grad_out + norm_back(grad_mixed_two * (1.0 + scale_two), normed_two, inv_two)
    mlp_layouts = (one_w_grad.shape, one_b_grad.shape, two_w_grad.shape, two_b_grad.shape)
    mlp_flat = lax.psum_scatter(
        pack_rows((one_w_grad, one_b_grad, two_w_grad, two_b_grad), group_size),
        ("fsdp", "seq"),
        scatter_dimension=0,
        tiled=True,
    )
    grad_branch = (gate_one * grad_resid).astype(jnp.bfloat16).reshape(token_rows, width)
    gate_one_grad = jnp.sum(grad_resid * branch_one, axis=1)
    out_w_grad = outer_dot(merged, grad_branch)
    out_b_grad = jnp.sum(grad_branch, axis=0, dtype=jnp.float32)
    grad_merged = back_dot(grad_branch, out_back).astype(jnp.bfloat16)
    grad_heads = grad_merged.reshape(latent_count, local_len, head_count, head_size).transpose(
        0, 2, 1, 3
    )
    grad_heads = grad_heads.reshape(latent_count, head_count, local_len * head_size)
    grad_heads = lax.all_to_all(grad_heads, "seq", split_axis=1, concat_axis=2, tiled=True)
    grad_heads = grad_heads.reshape(latent_count, local_heads, full_len, head_size)
    grad_queries, grad_keys, grad_vals = attention_backward(
        queries, key_rows, val_rows, log_totals, grad_heads
    )
    stacked = jnp.stack([grad_queries, grad_keys, grad_vals]).astype(jnp.bfloat16)
    stacked = stacked.reshape(3, latent_count, local_heads, full_len * head_size)
    grad_tokens = lax.all_to_all(stacked, "seq", split_axis=3, concat_axis=2, tiled=True)
    grad_proj = grad_tokens.reshape(3, latent_count, head_count, local_len, head_size).transpose(
        1, 3, 0, 2, 4
    )
    grad_proj = grad_proj.reshape(token_rows, 3 * width)
    qkv_w_grad = outer_dot(mixed_one, grad_proj)
    proj_sums = jnp.sum(grad_proj, axis=0, dtype=jnp.float32)
    qv_b_grad = jnp.concatenate([proj_sums[:width], proj_sums[2 * width :]])
    grad_mixed_one = back_dot(grad_proj, qkv_back).reshape(latent_count, local_len, width)
    shift_one_grad = jnp.sum(grad_mixed_one, axis=1)
    scale_one_grad = jnp.sum(grad_mixed_one * normed_one, axis=1)
    grad_inputs = grad_resid + norm_back(grad_mixed_one * (1.0 + scale_one), normed_one, inv_one)
    partial_mod = jnp.concatenate(
        [
            shift_one_grad,
            scale_one_grad,
            gate_one_grad,
            shift_two_grad,
            scale_two_grad,
            gate_two_grad,
        ],
        axis=1,
    )
    mod_grad = lax.psum(partial_mod, "seq").astype(jnp.bfloat16)
    mod_every = lax.all_gather(mod_grad, ("rep", "fsdp"), axis=0, tiled=True)
    ada_w_grad = outer_dot(silu_owned, mod_every)
    ada_b_grad = jnp.sum(
        lax.dynamic_slice_in_dim(mod_every, owner * bias_cols, bias_cols, 1),
        axis=0,
        dtype=jnp.float32,
    )
    cond_part = back_dot(mod_every, w_ada)
    cond_every = lax.all_gather(cond_part, ("fsdp", "seq"), axis=1, tiled=True)
    cond_lin = lax.dynamic_slice_in_dim(cond_every, first_latent, latent_count, 0)
    cond_grad = cond_lin * cond_sigmoid * (1.0 + cond_float * (1.0 - cond_sigmoid))
    attn_layouts = (qkv_w_grad.shape, qv_b_grad.shape, out_w_grad.shape, out_b_grad.shape)
    attn_flat = lax.psum_scatter(
        pack_rows((qkv_w_grad, qv_b_grad, out_w_grad, out_b_grad), group_size),
        ("fsdp", "seq"),
        scatter_dimension=0,
        tiled=True,
    )
    attn_total, mlp_total = (
        lax.psum(attn_flat.astype(jnp.bfloat16), "rep").astype(jnp.float32),
        lax.psum(mlp_flat.astype(jnp.bfloat16), "rep").astype(jnp.float32),
    )
    attn_parts = unpack_rows(attn_total, attn_layouts, group_size)
    mlp_parts = unpack_rows(mlp_total, mlp_layouts, group_size)
    return (
        block_out,
        grad_inputs,
        cond_grad,
        ada_w_grad,
        ada_b_grad,
        attn_parts[0],
        attn_parts[1],
        attn_parts[2],
        attn_parts[3],
        mlp_parts[0],
        mlp_parts[1],
        mlp_parts[2],
        mlp_parts[3],
    )


def solution(mesh):
    in_specs = (
        P(("rep", "fsdp"), "seq", None),
        P(("rep", "fsdp"), None),
        P(("fsdp", "seq"), None),
        P(("fsdp", "seq")),
        P(("fsdp", "seq"), None),
        P(("fsdp", "seq")),
        P(("fsdp", "seq"), None),
        P(("fsdp", "seq")),
        P(("fsdp", "seq"), None),
        P(("fsdp", "seq")),
        P(("fsdp", "seq"), None),
        P(("fsdp", "seq")),
        P(("rep", "fsdp"), "seq", None),
    )
    out_specs = (
        P(("rep", "fsdp"), "seq", None),
        P(("rep", "fsdp"), "seq", None),
        P(("rep", "fsdp"), None),
        P(("fsdp", "seq"), None),
        P(("fsdp", "seq")),
        P(("fsdp", "seq"), None),
        P(("fsdp", "seq")),
        P(("fsdp", "seq"), None),
        P(("fsdp", "seq")),
        P(("fsdp", "seq"), None),
        P(("fsdp", "seq")),
        P(("fsdp", "seq"), None),
        P(("fsdp", "seq")),
    )
    return jax.shard_map(
        on_device, mesh=mesh, in_specs=in_specs, out_specs=out_specs, check_vma=False
    )
```

profile of v0, /device:TPU:0, one launch (start us, length us, event | category | flops | bytes accessed | tf_op | source)
XLA Modules:
  0.0 3231.1 jit_solution(2037017178745607638)
XLA Ops:
  8.7 32.3 %all-gather = bf16[8,1,1152]{2,1,0:T(2,128)(2,1)S(1)} all-gather(bf16[1,1,1152]{2,1,0:T(2,128)(2,1)S(1)} %get-tuple-element.247), channel_id=1, replica_groups=mesh['rep'=2,'fsdp'=4,'seq'=4] {'rep','fsdp'}, dimensions={0}, use_global_device_ids=true | all-gather | bytes 20736 | tf_op jit(solution)/shard_map/all_gather | solution.py:171
  50.0 57.8 %all-reduce.7 = (bf16[2304]{0:T(1024)(128)(2,1)S(1)}, bf16[1152]{0:T(1024)(128)(2,1)S(1)}, bf16[1152]{0:T(1024)(128)(2,1)S(1)}, bf16[4608]{0:T(1024)(128)(2,1)S(1)}) all-reduce(bf16[2304]{0:T(1024)(128)(2,1)S(1)} %dynamic-update-slice, bf16[1152]{0:T(1024)(128)(2,1)S(1)} %dynamic-update-slice.1, ...), channel_id=1, replica_groups=mesh['rep'=2,'fsdp'=4,'seq'=4] {'fsdp','seq'}, use_global_device_ids=true, to_apply=%add | all-reduce | flops 9216 | bytes 36864
  108.3 25.0 all-reduce.13.cloned.1.call-done
  134.9 73.7 %all-gather.8.cloned.1.call-done = bf16[1152,3456]{1,0:T(8,128)(2,1)} async-done(((bf16[72,3456]{1,0:T(8,128)(2,1)}), bf16[1152,3456]{1,0:T(8,128)(2,1)}) %all-gather.8.cloned.1.call-update) | async-done | bytes 7962640 | tf_op jit(solution)/shard_map/all_gather | solution.py:185
  233.5 35.5 %all-to-all-done = bf16[3,1,16,18432]{3,0,1,2:T(4,128)(2,1)S(1)} async-done(((bf16[3,1,16,18432]{3,0,1,2:T(4,128)(2,1)}), bf16[3,1,16,18432]{3,0,1,2:T(4,128)(2,1)S(1)}, u32[]{:S(2)}, u32[]{:S(2)}) %all-to-all-start) | async-done | bytes 1769504 | tf_op jit(solution)/shard_map/all_to_all | solution.py:208
  299.4 56.5 %copy.113 = bf16[1,4,73728]{1,0,2:T(2,128)(2,1)} copy(bf16[1,4,73728]{2,1,0:T(4,128)(2,1)S(1)} %reshape_reshape.6) | data formatting | bytes 1179648 | tf_op jit(solution)/shard_map/reshape;reshape | solution.py:215
  356.5 400.0 %reduce.40 = bf16[73728,4]{1,0:T(8,128)(2,1)} reduce(bf16[73728,1,4]{2,1,0:T(2,128)(2,1)} %bitcast.242, bf16[]{:T(256)} %broadcast.232), dimensions={1}, to_apply=%bitcast.165.reduce_sub_computation | reduce | bytes 1179650
  756.5 51.0 %reshape.503 = bf16[4,2,36864]{2,1,0:T(2,128)(2,1)} reshape(bf16[73728,4]{1,0:T(8,128)(2,1)} %reduce.40) | data formatting | bytes 1179648
  821.7 61.7 %reshape.504 = bf16[73728,1,4]{2,1,0:T(2,128)(2,1)} reshape(bf16[4,2,36864]{2,1,0:T(2,128)(2,1)} %all-to-all-done.1) | data formatting | bytes 1179648
  883.4 69.2 %copy.114 = bf16[1,4,73728]{2,1,0:T(4,128)(2,1)} copy(bf16[1,4,73728]{1,0,2:T(2,128)(2,1)} %bitcast.243) | data formatting | bytes 1179648 | tf_op jit(solution)/shard_map/all_to_all | solution.py:214
  1041.6 19.7 reshape.451
  1105.1 38.5 %while.28 = (s32[]{:T(128)}, f32[1,4,1024,72]{2,3,1,0:T(8,128)}, f32[1,4,1024,72]{2,3,1,0:T(8,128)S(1)}, bf16[2,1,4,512,72]{3,4,2,1,0:T(8,128)(2,1)}, bf16[2,1,4...) while((s32[]{:T(128)}, f32[1,4,1024,72]{2,3,1,0:T(8,128)}, ...), condition=%wide.region_13.14_spmd.clone, body=%wide.region_11.13_spmd.clone.sunk | while | flops 1536735232 | bytes 133357912 | solution.py:149
  1159.2 70.1 %copy.128 = bf16[3,1,4,73728]{2,0,1,3:T(4,128)(2,1)} copy(bf16[3,1,4,73728]{3,2,1,0:T(4,128)(2,1)S(1)} %pad_maximum_fusion) | data formatting | bytes 3538944 | tf_op jit(solution)/shard_map/stack | solution.py:287
  1229.2 89.9 %reshape.507 = bf16[4,2,110592]{2,1,0:T(2,128)(2,1)} reshape(bf16[73728,1,3,4]{3,2,1,0:T(4,128)(2,1)} %bitcast.169) | data formatting | bytes 3538944
  1336.6 19.7 reshape.453
  1357.8 57.9 %dynamic-update-slice.6 = f32[16,663912]{1,0:T(8,128)} dynamic-update-slice(f32[16,663912]{1,0:T(8,128)} %dynamic-update-slice.5, f32[16,331776]{1,0:T(8,128)} %reshape.453, s32[]{} %constant.143, s32[]{} %constant.145) | dynamic-update-slice | bytes 42467332
  1417.2 56.3 %reshape.455 = f32[10622592]{0:T(1024)} reshape(f32[16,663912]{1,0:T(8,128)} %dynamic-update-slice.7) | data formatting | bytes 84980736 | tf_op jit(solution)/shard_map/reshape | solution.py:54
  1473.5 102.3 %reshape.508 = bf16[73728,1,3,4]{3,2,1,0:T(4,128)(2,1)} reshape(bf16[4,2,110592]{2,1,0:T(2,128)(2,1)S(1)} %all-to-all-done.3) | data formatting | bytes 3538944
  1575.8 101.6 %copy.134 = bf16[3,1,4,4,18432]{4,3,2,0,1:T(4,128)(2,1)} copy(bf16[3,1,4,4,18432]{2,0,4,3,1:T(4,128)(2,1)} %bitcast.33) | data formatting | bytes 3538944 | tf_op jit(solution)/shard_map/all_to_all | solution.py:289
  1755.2 26.6 reshape.448
  1781.8 1341.9 %all-reduce.16 = (bf16[5311872]{0:T(1024)(128)(2,1)}, bf16[10622592]{0:T(1024)(128)(2,1)}) all-reduce(f32[5311872]{0:T(1024)} %reshape.448, f32[10622592]{0:T(1024)} %reshape.455), channel_id=2, replica_groups=mesh['rep'=2,'fsdp'=4,'seq'=4] {'fsdp','seq'}, use_global_device_ids=true, to_apply=%region_26.27.clone | all-reduce | flops 15934464 | bytes 95606784
  3132.6 22.9 psum.29
  3155.6 31.3 all-gather.1
  3187.2 18.8 all-gather.2
  (308 shorter events, 401.8 us)
Async XLA Ops:
  7.2 41.8 %copy-start.53 = (bf16[72]{0:T(256)(128)(2,1)S(1)}, bf16[72]{0:T(256)(128)(2,1)}, u32[]{:S(2)}) copy-start(bf16[72]{0:T(256)(128)(2,1)} %param.24) | copy-start | bytes 436
  7.2 42.0 %copy-start.54 = (bf16[72]{0:T(256)(128)(2,1)S(1)}, bf16[72]{0:T(256)(128)(2,1)}, u32[]{:S(2)}) copy-start(bf16[72]{0:T(256)(128)(2,1)} %param.28) | copy-start | bytes 436
  7.2 42.3 %copy-start.55 = (bf16[144]{0:T(256)(128)(2,1)S(1)}, bf16[144]{0:T(256)(128)(2,1)}, u32[]{:S(2)}) copy-start(bf16[144]{0:T(256)(128)(2,1)} %param.22) | copy-start | bytes 868
  7.2 42.5 %copy-start.52 = (bf16[288]{0:T(512)(128)(2,1)S(1)}, bf16[288]{0:T(512)(128)(2,1)}, u32[]{:S(2)}) copy-start(bf16[288]{0:T(512)(128)(2,1)} %param.26) | copy-start | bytes 1732
  7.2 100.5 %copy-start.10 = (bf16[1,256,1152]{2,1,0:T(8,128)(2,1)S(1)}, bf16[1,256,1152]{2,1,0:T(8,128)(2,1)}, u32[]{:S(2)}) copy-start(bf16[1,256,1152]{2,1,0:T(8,128)(2,1)} %param.17) | copy-start | bytes 1769476
  7.3 126.1 %all-reduce.13.cloned.1.call-start = ((), (), s32[]{:S(2)}) async-start(), calls=%async_computation.4 | async-start | bytes 442368 | tf_op jit(solution)/shard_map/psum | solution.py:179
  43.8 164.9 %all-gather.8.cloned.1.call-start = ((), (), s32[]{:S(2)}) async-start(), calls=%async_computation.5 | async-start | bytes 8460288 | tf_op jit(solution)/shard_map/all_gather | solution.py:185
  44.5 919.2 %all-gather.10.cloned.1.call-start = ((), (), s32[]{:S(2)}) async-start(), calls=%async_computation.6 | async-start | bytes 2820096 | tf_op jit(solution)/shard_map/all_gather | solution.py:187
  45.2 923.9 %all-gather.12.cloned.1.call-start = ((), (), s32[]{:S(2)}) async-start(), calls=%async_computation.7 | async-start | bytes 11280384 | tf_op jit(solution)/shard_map/all_gather | solution.py:189
  45.8 933.3 %all-gather.14.cloned.1.call-start = ((), (), s32[]{:S(2)}) async-start(), calls=%async_computation.8 | async-start | bytes 11280384 | tf_op jit(solution)/shard_map/all_gather | solution.py:191
  108.0 100.7 %copy-start.38 = (f32[256]{0:T(256)}, f32[256]{0:T(256)S(1)}, u32[]{:S(2)}) copy-start(f32[256]{0:T(256)S(1)} %broadcast_multiply_fusion.5) | copy-start | bytes 3076
  108.3 100.4 %copy-start.42 = (f32[256]{0:T(256)}, f32[256]{0:T(256)S(1)}, u32[]{:S(2)}) copy-start(f32[256]{0:T(256)S(1)} %add_rsqrt_fusion.1) | copy-start | bytes 3076
  134.9 73.7 %copy-start.27 = (f32[1152]{0:T(1024)}, f32[1152]{0:T(1024)S(1)}, u32[]{:S(2)}) copy-start(f32[1152]{0:T(1024)S(1)} %get-tuple-element.202) | copy-start | bytes 13828
  134.9 73.7 %copy-start.30 = (f32[1152]{0:T(1024)}, f32[1152]{0:T(1024)S(1)}, u32[]{:S(2)}) copy-start(f32[1152]{0:T(1024)S(1)} %get-tuple-element.201) | copy-start | bytes 13828
  229.4 39.6 %all-to-all-start = ((bf16[3,1,16,18432]{3,0,1,2:T(4,128)(2,1)}), bf16[3,1,16,18432]{3,0,1,2:T(4,128)(2,1)S(1)}, u32[]{:S(2)}, u32[]{:S(2)}) async-start(bf16[3,1,16,18432]{3,0,1,2:T(4,128)(2,1)} %reshape.492), calls=%async_computation | async-start | bytes 4718592 | tf_op jit(solution)/shard_map/all_to_all | solution.py:208
  294.9 61.0 %copy-start.4 = (bf16[1,4,1024,72]{2,3,1,0:T(8,128)(2,1)}, bf16[1,4,1024,72]{2,3,1,0:T(8,128)(2,1)S(1)}, u32[]{:S(2)}) copy-start(bf16[1,4,1024,72]{2,3,1,0:T(8,128)(2,1)S(1)} %get-tuple-element.443) | copy-start | bytes 1769476
  294.9 61.0 %copy-start.33 = (f32[2,1,4,512]{3,2,1,0:T(4,128)}, f32[2,1,4,512]{3,2,1,0:T(4,128)S(1)}, u32[]{:S(2)}) copy-start(f32[2,1,4,512]{3,2,1,0:T(4,128)S(1)} %get-tuple-element.405) | copy-start | bytes 49156
  807.5 14.2 all-to-all-start.1
  1037.0 48.5 %all-to-all-start.2 = ((bf16[4,2,36864]{2,1,0:T(2,128)(2,1)}), bf16[4,2,36864]{2,1,0:T(2,128)(2,1)}, u32[]{:S(2)}, u32[]{:S(2)}) async-start(bf16[4,2,36864]{2,1,0:T(2,128)(2,1)} %reshape.505), calls=%async_computation.2 | async-start | bytes 1179648 | tf_op jit(solution)/shard_map/all_to_all | solution.py:282
  1319.1 154.4 %all-to-all-start.3 = ((bf16[4,2,110592]{2,1,0:T(2,128)(2,1)}), bf16[4,2,110592]{2,1,0:T(2,128)(2,1)S(1)}, u32[]{:S(2)}, u32[]{:S(2)}) async-start(bf16[4,2,110592]{2,1,0:T(2,128)(2,1)} %reshape.507), calls=%async_computation.3 | async-start | bytes 3538944 | tf_op jit(solution)/shard_map/all_to_all | solution.py:289
  1322.9 1886.3 %all-reduce.15.cloned.1.call-start = ((), (), s32[]{:S(2)}) async-start(), calls=%async_computation.9 | async-start | bytes 3989504 | tf_op jit(solution)/shard_map/psum | solution.py:332
  3129.3 77.6 %copy-start.47 = (bf16[8,1,72]{2,1,0:T(2,128)(2,1)S(1)}, bf16[8,1,72]{2,1,0:T(2,128)(2,1)}, u32[]{:S(2)}) copy-start(bf16[8,1,72]{2,1,0:T(2,128)(2,1)} %copy-done.46) | copy-start | bytes 3460
  3132.5 76.1 %copy-start.44 = (bf16[1,1152]{1,0:T(2,128)(2,1)S(1)}, bf16[1,1152]{1,0:T(2,128)(2,1)}, u32[]{:S(2)}) copy-start(bf16[1,1152]{1,0:T(2,128)(2,1)} %param.18) | copy-start | bytes 6916
  3132.5 76.1 %copy-start.45 = (f32[1,1152]{1,0:T(1,128)S(1)}, f32[1,1152]{1,0:T(1,128)}, u32[]{:S(2)}) copy-start(f32[1,1152]{1,0:T(1,128)} %get-tuple-element.248) | copy-start | bytes 13828
  (49 other events, 322.6 us)
Sparse Core Ops, SparseCore 0:
  43.9 89.4 all-reduce.12
  135.5 73.1 all-gather.7
  210.8 48.3 all-gather.9
  261.4 87.6 all-gather.11
  351.2 86.8 all-gather.13
  3129.4 68.6 all-reduce.14
where the time goes:
time: 3250 us; the launch traced here: 3230 us
  blocking collectives  1510 us (46%)
  local copies, waits for them, and re-layouts  984 us (30%)
  other arithmetic  434 us (13%)
  waiting for transfers between devices  145 us (4%)
  matrix products  128 us (4%)
    unnamed x2, blocking collectives  1400 us
    unnamed x127, local copies, waits for them, and re-layouts  428 us
    unnamed x5, other arithmetic  407 us
    all_to_all x2, local copies, waits for them, and re-layouts, on_device(): lax.all_to_all(stacked, 'seq', split_axis=3, concat_axis=2, tiled=True)  104 us
    reshape x2, local copies, waits for them, and re-layouts, pack_rows(): jnp.concatenate([array.reshape(groups, -1) for array in arrays], axis=1)  82.9 us
    another operation x4, local copies, waits for them, and re-layouts, on_device(): jnp.stack([grad_queries, grad_keys, grad_vals]).astype(jnp.bfloat16)  78 us
    all_to_all x3, local copies, waits for them, and re-layouts, on_device(): lax.all_to_all(attended.reshape(latent_count, local_heads, full_len * hea...  73.9 us
    all_gather x1, waiting for transfers between devices, on_device(): lax.all_gather(w_qkv, ('fsdp', 'seq'), axis=0, tiled=True)  73.7 us
  transfers between devices with their start and end apart: 10, of which 4 were waited for; matrix products, arithmetic and copies ran while one was open for 28% of the time, Pallas kernels for 0%

commit v1 on v0

--- a/solution.py
+++ b/solution.py
@@ -7,6 +7,20 @@
 H = 16
 epsilon = 1e-06
 gelu_coef = math.sqrt(2.0 / math.pi)
+
+
+def drive_table_in(block_here, dim_i, arr):
+    r2 = block_here.shape
+    opened = block_here.reshape(*r2[:dim_i], arr, r2[dim_i] // arr, *r2[dim_i + 1 :])
+    prior = jnp.moveaxis(opened, dim_i, 0)
+    return prior
+
+
+def target_note(frame_in, d0):
+    frame_in = jnp.moveaxis(frame_in, 0, d0)
+    then = frame_in.shape
+    response = frame_in.reshape(*then[:d0], then[d0] * then[d0 + 1], *then[d0 + 2 :])
+    return response
 
 
 def norm_stats(values):
@@ -286,7 +300,14 @@
     )
     stacked = jnp.stack([grad_queries, grad_keys, grad_vals]).astype(jnp.bfloat16)
     stacked = stacked.reshape(3, latent_count, local_heads, full_len * head_size)
-    grad_tokens = lax.all_to_all(stacked, "seq", split_axis=3, concat_axis=2, tiled=True)
+    z_new, all_rows = (lax.axis_size("seq"), lax.axis_index("seq"))
+    block_now = drive_table_in(stacked, 3, z_new)
+    entries = [block_now[all_rows]]
+    for d in range(1, z_new):
+        carry_in = block_now[all_rows ^ d]
+        entries.append(lax.ppermute(carry_in, "seq", [(s, s ^ d) for s in range(z_new)]))
+    block_now = jnp.stack(entries, axis=0)[all_rows ^ jnp.arange(z_new)]
+    grad_tokens = target_note(block_now, 2)
     grad_proj = grad_tokens.reshape(3, latent_count, head_count, local_len, head_size).transpose(
         1, 3, 0, 2, 4
     )

time: 3250 us -> 2890 us (0.89)
  local copies, waits for them, and re-layouts: 984 us -> 640 us
    unnamed x127 -> x137, local copies, waits for them, and re-layouts: 428 us -> 242 us
    all_to_all x2 -> x0, local copies, waits for them, and re-layouts: 104 us -> none  [on_device(): lax.all_to_all(stacked, 'seq', split_axis=3, concat_axis=2, tiled=True)]
    another operation x4, local copies, waits for them, and re-layouts: 78 us -> 11.9 us  [on_device(): jnp.stack([grad_queries, grad_keys, grad_vals]).astype(jnp.bfloat16)]
    unnamed x5 -> x6, other arithmetic: 407 us -> 407 us
  transfers between devices with their start and end apart: 10 -> 12, of which waited for: 4 -> 4; matrix products, arithmetic and copies ran while one was open for 28% -> 32% of each run, Pallas kernels for 0% -> 0%
where the time goes in v1:
time: 2890 us; the launch traced here: 2880 us
  blocking collectives  1500 us (52%)
  local copies, waits for them, and re-layouts  640 us (22%)
  other arithmetic  435 us (15%)
  waiting for transfers between devices  144 us (5%)
  matrix products  124 us (4%)
    unnamed x2, blocking collectives  1390 us
    unnamed x6, other arithmetic  407 us
    unnamed x137, local copies, waits for them, and re-layouts  242 us
    reshape x2, local copies, waits for them, and re-layouts, pack_rows(): jnp.concatenate([array.reshape(groups, -1) for array in arrays], axis=1)  82.8 us
    all_to_all x3, local copies, waits for them, and re-layouts, on_device(): lax.all_to_all(attended.reshape(latent_count, local_heads, full_len * hea...  73.9 us
    all_gather x1, waiting for transfers between devices, on_device(): lax.all_gather(w_qkv, ('fsdp', 'seq'), axis=0, tiled=True)  73.7 us
    reshape x7, local copies, waits for them, and re-layouts, pack_rows(): array.reshape(groups, -1)  59.6 us
    another operation x2, local copies, waits for them, and re-layouts, on_device(): attended.reshape(latent_count, local_heads, full_len * head_size)  59.5 us
  transfers between devices with their start and end apart: 12, of which 4 were waited for; matrix products, arithmetic and copies ran while one was open for 32% of the time, Pallas kernels for 0%

profile of v1, /device:TPU:0, one launch (start us, length us, event | category | flops | bytes accessed | tf_op | source)
XLA Modules:
  0.0 2876.9 jit_solution(3698009586870991052)
XLA Ops:
  8.6 32.3 %all-gather = bf16[8,1,1152]{2,1,0:T(2,128)(2,1)S(1)} all-gather(bf16[1,1,1152]{2,1,0:T(2,128)(2,1)S(1)} %get-tuple-element.232), channel_id=1, replica_groups=mesh['rep'=2,'fsdp'=4,'seq'=4] {'rep','fsdp'}, dimensions={0}, use_global_device_ids=true | all-gather | bytes 20736 | tf_op jit(solution)/shard_map/all_gather | solution.py:185
  50.0 57.8 %all-reduce.7 = (bf16[2304]{0:T(1024)(128)(2,1)S(1)}, bf16[1152]{0:T(1024)(128)(2,1)S(1)}, bf16[1152]{0:T(1024)(128)(2,1)S(1)}, bf16[4608]{0:T(1024)(128)(2,1)S(1)}) all-reduce(bf16[2304]{0:T(1024)(128)(2,1)S(1)} %dynamic-update-slice, bf16[1152]{0:T(1024)(128)(2,1)S(1)} %dynamic-update-slice.1, ...), channel_id=1, replica_groups=mesh['rep'=2,'fsdp'=4,'seq'=4] {'fsdp','seq'}, use_global_device_ids=true, to_apply=%add | all-reduce | flops 9216 | bytes 36864
  108.2 25.0 all-reduce.13.cloned.1.call-done
  134.9 73.7 %all-gather.8.cloned.1.call-done = bf16[1152,3456]{1,0:T(8,128)(2,1)} async-done(((bf16[72,3456]{1,0:T(8,128)(2,1)}), bf16[1152,3456]{1,0:T(8,128)(2,1)}) %all-gather.8.cloned.1.call-update) | async-done | bytes 7962640 | tf_op jit(solution)/shard_map/all_gather | solution.py:199
  233.5 35.5 %all-to-all-done = bf16[3,1,16,18432]{3,0,1,2:T(4,128)(2,1)S(1)} async-done(((bf16[3,1,16,18432]{3,0,1,2:T(4,128)(2,1)}), bf16[3,1,16,18432]{3,0,1,2:T(4,128)(2,1)S(1)}, u32[]{:S(2)}, u32[]{:S(2)}) %all-to-all-start) | async-done | bytes 1769504 | tf_op jit(solution)/shard_map/all_to_all | solution.py:222
  283.6 11.3 while.27
  299.4 56.5 %copy.83 = bf16[1,4,73728]{1,0,2:T(2,128)(2,1)} copy(bf16[1,4,73728]{2,1,0:T(4,128)(2,1)S(1)} %reshape_reshape.10) | data formatting | bytes 1179648 | tf_op jit(solution)/shard_map/reshape;reshape | solution.py:229
  356.4 400.1 %reduce.40 = bf16[73728,4]{1,0:T(8,128)(2,1)} reduce(bf16[73728,1,4]{2,1,0:T(2,128)(2,1)} %bitcast.260, bf16[]{:T(256)} %broadcast.267), dimensions={1}, to_apply=%bitcast.181.reduce_sub_computation | reduce | bytes 1179650
  756.5 51.0 %reshape.530 = bf16[4,2,36864]{2,1,0:T(2,128)(2,1)} reshape(bf16[73728,4]{1,0:T(8,128)(2,1)} %reduce.40) | data formatting | bytes 1179648
  821.7 61.6 %reshape.531 = bf16[73728,1,4]{2,1,0:T(2,128)(2,1)} reshape(bf16[4,2,36864]{2,1,0:T(2,128)(2,1)} %all-to-all-done.1) | data formatting | bytes 1179648
  883.3 69.2 %copy.84 = bf16[1,4,73728]{2,1,0:T(4,128)(2,1)} copy(bf16[1,4,73728]{1,0,2:T(2,128)(2,1)} %bitcast.261) | data formatting | bytes 1179648 | tf_op jit(solution)/shard_map/all_to_all | solution.py:228
  1041.5 20.1 reshape.468
  1061.7 14.9 constant_dynamic-update-slice_fusion.10
  1096.2 38.7 %while.28 = (s32[]{:T(128)}, f32[1,4,1024,72]{2,3,1,0:T(8,128)}, f32[1,4,1024,72]{2,3,1,0:T(8,128)S(1)}, bf16[2,1,4,512,72]{3,4,2,1,0:T(8,128)(2,1)}, bf16[2,1,4...) while((s32[]{:T(128)}, f32[1,4,1024,72]{2,3,1,0:T(8,128)}, ...), condition=%wide.region_13.14_spmd.clone, body=%wide.region_11.13_spmd.clone.sunk | while | flops 1536735232 | bytes 133357912 | solution.py:163
  1184.3 19.7 reshape.470
  1205.5 57.9 %dynamic-update-slice.6 = f32[16,663912]{1,0:T(8,128)} dynamic-update-slice(f32[16,663912]{1,0:T(8,128)} %dynamic-update-slice.5, f32[16,331776]{1,0:T(8,128)} %reshape.470, s32[]{} %constant.151, s32[]{} %constant.153) | dynamic-update-slice | bytes 42467332
  1265.2 56.2 %reshape.472 = f32[10622592]{0:T(1024)} reshape(f32[16,663912]{1,0:T(8,128)} %dynamic-update-slice.7) | data formatting | bytes 84980736 | tf_op jit(solution)/shard_map/reshape | solution.py:68
  1360.8 15.1 reshape.462
  1388.5 16.0 dynamic-update-slice.10
  1406.0 26.6 reshape.465
  1432.6 1335.6 %all-reduce.16 = (bf16[5311872]{0:T(1024)(128)(2,1)}, bf16[10622592]{0:T(1024)(128)(2,1)}) all-reduce(f32[5311872]{0:T(1024)} %reshape.465, f32[10622592]{0:T(1024)} %reshape.472), channel_id=2, replica_groups=mesh['rep'=2,'fsdp'=4,'seq'=4] {'fsdp','seq'}, use_global_device_ids=true, to_apply=%region_26.27.clone | all-reduce | flops 15934464 | bytes 95606784
  2777.2 23.4 psum.29
  2800.5 31.2 %all-gather.1 = bf16[8,1,6912]{2,1,0:T(2,128)(2,1)S(1)} all-gather(bf16[1,1,6912]{2,1,0:T(2,128)(2,1)S(1)} %bitcast.286), channel_id=1, replica_groups=mesh['rep'=2,'fsdp'=4,'seq'=4] {'rep','fsdp'}, dimensions={0}, use_global_device_ids=true | all-gather | bytes 124416 | tf_op jit(solution)/shard_map/all_gather | solution.py:334
  2832.1 19.7 all-gather.2
  (326 shorter events, 358.9 us)
Async XLA Ops:
  7.2 35.1 %copy-start = (bf16[72,6912]{1,0:T(8,128)(2,1)S(1)}, bf16[72,6912]{1,0:T(8,128)(2,1)}, u32[]{:S(2)}) copy-start(bf16[72,6912]{1,0:T(8,128)(2,1)} %param.19) | copy-start | bytes 2985988
  7.2 126.1 %all-reduce.13.cloned.1.call-start = ((), (), s32[]{:S(2)}) async-start(), calls=%async_computation.3 | async-start | bytes 442368 | tf_op jit(solution)/shard_map/psum | solution.py:193
  42.3 65.4 %copy-start.10 = (bf16[1,256,1152]{2,1,0:T(8,128)(2,1)S(1)}, bf16[1,256,1152]{2,1,0:T(8,128)(2,1)}, u32[]{:S(2)}) copy-start(bf16[1,256,1152]{2,1,0:T(8,128)(2,1)} %param.17) | copy-start | bytes 1769476
  43.7 164.9 %all-gather.8.cloned.1.call-start = ((), (), s32[]{:S(2)}) async-start(), calls=%async_computation.4 | async-start | bytes 8460288 | tf_op jit(solution)/shard_map/all_gather | solution.py:199
  44.5 919.1 %all-gather.10.cloned.1.call-start = ((), (), s32[]{:S(2)}) async-start(), calls=%async_computation.5 | async-start | bytes 2820096 | tf_op jit(solution)/shard_map/all_gather | solution.py:201
  45.2 923.8 %all-gather.12.cloned.1.call-start = ((), (), s32[]{:S(2)}) async-start(), calls=%async_computation.6 | async-start | bytes 11280384 | tf_op jit(solution)/shard_map/all_gather | solution.py:203
  45.8 933.1 %all-gather.14.cloned.1.call-start = ((), (), s32[]{:S(2)}) async-start(), calls=%async_computation.7 | async-start | bytes 11280384 | tf_op jit(solution)/shard_map/all_gather | solution.py:205
  107.9 100.7 %copy-start.38 = (f32[256]{0:T(256)}, f32[256]{0:T(256)S(1)}, u32[]{:S(2)}) copy-start(f32[256]{0:T(256)S(1)} %broadcast_multiply_fusion.5) | copy-start | bytes 3076
  108.2 100.4 %copy-start.42 = (f32[256]{0:T(256)}, f32[256]{0:T(256)S(1)}, u32[]{:S(2)}) copy-start(f32[256]{0:T(256)S(1)} %add_rsqrt_fusion.1) | copy-start | bytes 3076
  134.9 73.7 %copy-start.31 = (f32[1152]{0:T(1024)}, f32[1152]{0:T(1024)S(1)}, u32[]{:S(2)}) copy-start(f32[1152]{0:T(1024)S(1)} %get-tuple-element.187) | copy-start | bytes 13828
  134.9 73.7 %copy-start.34 = (f32[1152]{0:T(1024)}, f32[1152]{0:T(1024)S(1)}, u32[]{:S(2)}) copy-start(f32[1152]{0:T(1024)S(1)} %get-tuple-element.186) | copy-start | bytes 13828
  229.4 39.6 %all-to-all-start = ((bf16[3,1,16,18432]{3,0,1,2:T(4,128)(2,1)}), bf16[3,1,16,18432]{3,0,1,2:T(4,128)(2,1)S(1)}, u32[]{:S(2)}, u32[]{:S(2)}) async-start(bf16[3,1,16,18432]{3,0,1,2:T(4,128)(2,1)} %reshape.519), calls=%async_computation | async-start | bytes 4718592 | tf_op jit(solution)/shard_map/all_to_all | solution.py:222
  294.9 61.0 %copy-start.4 = (bf16[1,4,1024,72]{2,3,1,0:T(8,128)(2,1)}, bf16[1,4,1024,72]{2,3,1,0:T(8,128)(2,1)S(1)}, u32[]{:S(2)}) copy-start(bf16[1,4,1024,72]{2,3,1,0:T(8,128)(2,1)S(1)} %get-tuple-element.432) | copy-start | bytes 1769476
  807.5 14.2 all-to-all-start.1
  1037.3 39.2 %all-to-all-start.2 = ((bf16[4,2,36864]{2,1,0:T(2,128)(2,1)}), bf16[4,2,36864]{2,1,0:T(2,128)(2,1)}, u32[]{:S(2)}, u32[]{:S(2)}) async-start(bf16[4,2,36864]{2,1,0:T(2,128)(2,1)} %reshape.532), calls=%async_computation.2 | async-start | bytes 1179648 | tf_op jit(solution)/shard_map/all_to_all | solution.py:296
  1041.5 1813.5 %all-reduce.15.cloned.1.call-start = ((), (), s32[]{:S(2)}) async-start(), calls=%async_computation.8 | async-start | bytes 3989504 | tf_op jit(solution)/shard_map/psum | solution.py:353
  1162.7 159.1 %collective-permute-start.2 = (bf16[3,1,4,18432]{3,2,0,1:T(4,128)(2,1)}, bf16[3,1,4,18432]{3,2,0,1:T(4,128)(2,1)S(1)}, u32[]{:S(2)}, u32[]{:S(2)}) collective-permute-start(bf16[3,1,4,18432]{3,2,0,1:T(4,128)(2,1)} %bitcast.220), channel_id=1, source_target_pairs={{0,3},{1,2},{2,1},{3,0},{4,7},{5,6},{6,5},{7,4},{8,11},{9,10},{10,... | collective-permute-start | bytes 1327112 | tf_op jit(solution)/shard_map/ppermute | solution.py:308
  1165.5 156.3 %collective-permute-start.1 = (bf16[3,1,4,18432]{3,2,0,1:T(4,128)(2,1)}, bf16[3,1,4,18432]{3,2,0,1:T(4,128)(2,1)S(1)}, u32[]{:S(2)}, u32[]{:S(2)}) collective-permute-start(bf16[3,1,4,18432]{3,2,0,1:T(4,128)(2,1)} %bitcast.221), channel_id=1, source_target_pairs={{0,2},{1,3},{2,0},{3,1},{4,6},{5,7},{6,4},{7,5},{8,10},{9,11},{10,... | collective-permute-start | bytes 1327112 | tf_op jit(solution)/shard_map/ppermute | solution.py:308
  1167.0 154.8 %collective-permute-start = (bf16[3,1,4,18432]{3,2,0,1:T(4,128)(2,1)}, bf16[3,1,4,18432]{3,2,0,1:T(4,128)(2,1)S(1)}, u32[]{:S(2)}, u32[]{:S(2)}) collective-permute-start(bf16[3,1,4,18432]{3,2,0,1:T(4,128)(2,1)} %bitcast.222), channel_id=1, source_target_pairs={{0,1},{1,0},{2,3},{3,2},{4,5},{5,4},{6,7},{7,6},{8,9},{9,8},{10,11... | collective-permute-start | bytes 1327112 | tf_op jit(solution)/shard_map/ppermute | solution.py:308
  1184.3 19.7 copy-start.40
  1265.2 56.2 %copy-start.18 = (bf16[3,1,4,1,18432]{4,3,2,1,0:T(2,128)(2,1)S(1)}, bf16[3,1,4,1,18432]{4,3,2,1,0:T(2,128)(2,1)}, u32[]{:S(2)}) copy-start(bf16[3,1,4,1,18432]{4,3,2,1,0:T(2,128)(2,1)} %get-tuple-element.238) | copy-start | bytes 1327108
  2777.0 75.6 %copy-start.48 = (bf16[8,1,72]{2,1,0:T(2,128)(2,1)S(1)}, bf16[8,1,72]{2,1,0:T(2,128)(2,1)}, u32[]{:S(2)}) copy-start(bf16[8,1,72]{2,1,0:T(2,128)(2,1)} %copy-done.47) | copy-start | bytes 3460
  2831.7 22.6 copy-start.45
  2831.7 22.6 copy-start.46
  (54 other events, 243.9 us)
Sparse Core Ops, SparseCore 0:
  43.8 89.4 all-reduce.12
  135.5 73.1 all-gather.7
  210.8 48.3 all-gather.9
  261.3 87.6 all-gather.11
  351.2 86.8 all-gather.13
  2773.9 72.1 all-reduce.14
